TPU v7x, 32 devices: a whole 2x2x4 slice. The times are simulated.
32 devices in a mesh: level: 2 (over y), sub: 16 (over z, x, core).
Axes of the slice: x: 2, y: 2, z: 4, core: 2. Of those that a mesh axis runs over, the one named last changes fastest.
Arguments:
- factor_inv: float32 [2, 16, 256, 256], P('level', 'sub'), may hold values from -0.0625 to 1.4, as said below
- update_blocks: float32 [2, 16, 4, 128, 256], P('level', 'sub'), may hold values from -0.1875 to 0.1875
- update_rows: int32 [2, 16, 4], P('level', 'sub'), may hold values from 0 to 3, each once within a row
- right_side: float32 [2, 16, 256, 512], P('level', 'sub'), may hold values from -4000 to 4000
Outputs:
- solution: float32 [2, 16, 256, 512], P('level', 'sub')
Inputs may be any that keep to these rules, and one draw needn't show every extreme that they name: `update_rows`: each supernode's 4 update blocks name the 4 target row blocks once each; values below 2 are row blocks of the parent supernode in the same subtree, the others those of the parent supernode in the next subtree (the last subtree's next is the first). `factor_inv`: each 256 x 256 block is lower triangular, with diagonal entries between 0.7 and 1.4.
All inputs are finite; a program needn't handle non-finite values.
Results may differ from a plain program's by a relative error of at most 0.00014.
Values sent between devices are 32-bit elements; how exact they have to be, the bound alone decides.
A program may use at most 64 MiB of HBM per device.

v0:
```python
import jax
import jax.numpy as jnp
from jax import lax
from jax.sharding import PartitionSpec as P

FULL_PRECISION = lax.Precision.HIGHEST


def passed_along(value, axis, steps):
    count = lax.axis_size(axis)
    pairs = [(source, (source + steps) % count) for source in range(count)]
    return lax.ppermute(value, axis, pairs)


def shifted(block, axis, distance):
    devices = range(lax.axis_size(axis))
    route = [(i - distance, i) for i in devices if i - distance in devices]
    return lax.ppermute(block, axis, route)


def apply_plain(matrix, values):
    return jnp.dot(matrix, values, precision=FULL_PRECISION, preferred_element_type=jnp.float32)


def apply_turned(matrix, values):
    return lax.dot_general(
        matrix,
        values,
        (((0,), (0,)), ((), ())),
        precision=FULL_PRECISION,
        preferred_element_type=jnp.float32,
    )


def per_device(factor_inv, update_blocks, update_rows, right_side):
    inverse = factor_inv[0, 0]
    sn_width = inverse.shape[0]
    blocks = update_blocks[0, 0]
    slot_count = blocks.shape[0]
    levels = lax.axis_size("level")
    my_level = lax.axis_index("level")
    slot_table = (
        update_rows[0, 0][:, None] == jnp.arange(slot_count, dtype=jnp.int32)[None, :]
    ).astype(jnp.float32)
    ordered = jnp.einsum("kd,kbj->dbj", slot_table, blocks, precision=FULL_PRECISION).reshape(
        slot_count * blocks.shape[1], sn_width
    )
    own_rows = ordered[:sn_width]
    next_rows = ordered[sn_width:]
    given_rhs = right_side[0, 0]
    partial_value = jnp.sum(given_rhs * given_rhs, axis=0)
    norm_total = lax.psum(partial_value, ("level", "sub"))
    col_scale = jnp.sqrt(norm_total / (levels * lax.axis_size("sub") * sn_width) + 1e-06)
    given_rhs = given_rhs / col_scale
    arrived = jnp.zeros_like(given_rhs)
    forward_all = jnp.zeros_like(given_rhs)
    for step_index in range(levels):
        forward_val = apply_plain(inverse, given_rhs - arrived)
        forward_all = jnp.where(my_level == step_index, forward_val, forward_all)
        if step_index + 1 < levels:
            spread = apply_plain(ordered, forward_val)
            from_left = passed_along(spread[sn_width:], "sub", 1)
            arrived = shifted(spread[:sn_width] + from_left, "level", 1)
    parent_x = jnp.zeros_like(given_rhs)
    result = jnp.zeros_like(given_rhs)
    for step_index in range(levels):
        rhs_block = forward_all
        if step_index > 0:
            beside = passed_along(parent_x, "sub", -1)
            rhs_block = rhs_block - (
                apply_turned(own_rows, parent_x) + apply_turned(next_rows, beside)
            )
        solved = apply_turned(inverse, rhs_block)
        result = jnp.where(my_level == levels - 1 - step_index, solved, result)
        if step_index + 1 < levels:
            parent_x = shifted(solved, "level", -1)
    return result[None, None]


def solution(mesh):
    return jax.shard_map(
        per_device,
        mesh=mesh,
        in_specs=(
            P("level", "sub", None, None),
            P("level", "sub", None, None, None),
            P("level", "sub", None),
            P("level", "sub", None, None),
        ),
        out_specs=P("level", "sub", None, None),
        check_vma=False,
    )
```

profile of v0, /device:TPU:0, one launch (start us, length us, event | category | flops | bytes accessed | tf_op | source)
XLA Modules:
  0.0 98.4 jit_solution(13960839743965393671)
XLA Ops:
  0.0 1.2 %fusion.5 = f32[512]{0:T(512)S(1)} fusion(f32[1,1,256,512]{3,2,1,0:T(8,128)} %param.7), kind=kLoop, calls=%fused_computation.12 | loop fusion | flops 261632 | bytes 526336 | tf_op jit(solution)/shard_map/reduce_sum | solution.py:51
  1.2 42.0 %psum.7 = f32[512]{0:T(512)S(1)} all-reduce(f32[512]{0:T(512)S(1)} %fusion.5), channel_id=1, replica_groups=mesh['level'=2,'sub'=16] {'level','sub'}, use_global_device_ids=true, to_apply=%region_1.0 | all-reduce | flops 512 | bytes 4096 | tf_op jit(solution)/shard_map/psum | solution.py:52
  43.2 0.6 copy-done.3
  43.9 0.9 fusion.8
  44.8 0.1 copy.8
  44.9 0.8 copy-done.1
  45.7 0.2 copy-done.2
  45.9 1.0 %fusion.3 = f32[512,256]{1,0:T(8,128)S(1)} fusion(f32[1,1,256,512]{3,2,1,0:T(8,128)S(1)} %copy-done.2, f32[1,1,256,256]{3,2,1,0:T(8,128)S(1)} %copy-done.1, f32[512]{0:T(512)S(1)} %add_sqrt_fusion), kind=kOutput, calls=%fused_computation.8 | convolution fusion | flops 402784256 | bytes 1312768 | tf_op jit(solution)/shard_map/dot_general | solution.py:22
  46.9 1.0 %fusion.21 = f32[512,512]{1,0:T(8,128)S(1)} fusion(f32[512,256]{1,0:T(8,128)S(1)} %bitcast.49, f32[512,256]{1,0:T(8,128)S(1)} %fusion.3), kind=kOutput, calls=%fused_computation.28 | convolution fusion | flops 805306368 | bytes 2097152 | tf_op jit(solution)/shard_map/dot_general | solution.py:22
  48.0 11.3 %collective-permute-done = f32[256,512]{1,0:T(8,128)S(1)} collective-permute-done((f32[256,512]{1,0:T(8,128)S(1)}, f32[256,512]{1,0:T(8,128)S(1)}, u32[]{:S(2)}, u32[]{:S(2)}) %collective-permute-start) | collective-permute-done | bytes 524320 | tf_op jit(solution)/shard_map/ppermute | solution.py:12
  59.3 0.1 slice_add_fusion
  59.4 4.2 %collective-permute-start.1 = (f32[256,512]{1,0:T(8,128)S(1)}, f32[256,512]{1,0:T(8,128)S(1)}, u32[]{:S(2)}, u32[]{:S(2)}) collective-permute-start(f32[256,512]{1,0:T(8,128)S(1)} %slice_add_fusion), channel_id=1, source_target_pairs={{0,16},{1,17},{2,18},{3,19},{4,20},{5,21},{6,22},{7,23},{8,24},{9,... | collective-permute-start | bytes 1572872 | tf_op jit(solution)/shard_map/ppermute | solution.py:18
  63.6 6.8 %collective-permute-done.1 = f32[256,512]{1,0:T(8,128)S(1)} collective-permute-done((f32[256,512]{1,0:T(8,128)S(1)}, f32[256,512]{1,0:T(8,128)S(1)}, u32[]{:S(2)}, u32[]{:S(2)}) %collective-permute-start.1) | collective-permute-done | bytes 524320 | tf_op jit(solution)/shard_map/ppermute | solution.py:18
  70.4 1.0 %convolution_select_fusion = f32[512,256]{1,0:T(8,128)S(1)} fusion(f32[256,512]{1,0:T(8,128)S(1)} %collective-permute-done.1, f32[1,1,256,512]{3,2,1,0:T(8,128)S(1)} %copy-done.2, f32[512,256]{1,0:T(8,128)S(1)} %fusion.3, f32[1,1,256,256]{3,2,1,0:T(8,128)S(1)} %copy-done.1, f32[512]{0:T(512)S(1)} %add_sqrt_fusion, pred[]{:T(512)S(6)} %eq.23, pred[]{:T(512)S(6)} %eq.24), kind=kOutput, calls=%fused_computation.4 | convolution fusion | flops 403177472 | bytes 2361346 | tf_op jit(solution)/shard_map/dot_general | solution.py:22
  71.4 0.6 convolution_bitcast_fusion.1
  72.0 1.3 %collective-permute-start.2 = (f32[256,512]{0,1:T(8,128)S(1)}, f32[256,512]{0,1:T(8,128)S(1)}, u32[]{:S(2)}, u32[]{:S(2)}) collective-permute-start(f32[256,512]{0,1:T(8,128)S(1)} %convolution_bitcast_fusion.1), channel_id=1, source_target_pairs={{16,0},{17,1},{18,2},{19,3},{20,4},{21,5},{22,6},{23,7},{24,8},{25... | collective-permute-start | bytes 1572872 | tf_op jit(solution)/shard_map/ppermute | solution.py:18
  73.3 9.8 %collective-permute-done.2 = f32[256,512]{0,1:T(8,128)S(1)} collective-permute-done((f32[256,512]{0,1:T(8,128)S(1)}, f32[256,512]{0,1:T(8,128)S(1)}, u32[]{:S(2)}, u32[]{:S(2)}) %collective-permute-start.2) | collective-permute-done | bytes 524320 | tf_op jit(solution)/shard_map/ppermute | solution.py:18
  83.1 6.5 %collective-permute-start.3 = (f32[256,512]{0,1:T(8,128)S(1)}, f32[256,512]{0,1:T(8,128)S(1)}, u32[]{:S(2)}, u32[]{:S(2)}) collective-permute-start(f32[256,512]{0,1:T(8,128)S(1)} %collective-permute-done.2), channel_id=1, source_target_pairs={{0,15},{1,0},{2,1},{3,2},{4,3},{5,4},{6,5},{7,6},{8,7},{9,8},{10,9... | collective-permute-start | bytes 1572872 | tf_op jit(solution)/shard_map/ppermute | solution.py:12
  89.6 0.2 fusion.20
  89.8 0.6 fusion.22
  90.4 5.8 %collective-permute-done.3 = f32[256,512]{0,1:T(8,128)S(1)} collective-permute-done((f32[256,512]{0,1:T(8,128)S(1)}, f32[256,512]{0,1:T(8,128)S(1)}, u32[]{:S(2)}, u32[]{:S(2)}) %collective-permute-start.3) | collective-permute-done | bytes 524320 | tf_op jit(solution)/shard_map/ppermute | solution.py:12
  96.3 0.6 fusion.2
  96.9 0.6 fusion.1
  97.4 1.0 %copy.11 = f32[1,1,256,512]{3,2,1,0:T(8,128)} copy(f32[1,1,256,512]{2,3,1,0:T(8,128)S(1)} %fusion.1) | data formatting | bytes 1048576 | tf_op jit(solution)/shard_map/broadcast_in_dim | solution.py:77
  (10 shorter events, 0.2 us)
Async XLA Ops:
  0.0 43.2 %copy-start = (f32[1,1,4,128,256]{4,3,2,1,0:T(8,128)S(1)}, f32[1,1,4,128,256]{4,3,2,1,0:T(8,128)}, u32[]{:S(2)}) copy-start(f32[1,1,4,128,256]{4,3,2,1,0:T(8,128)} %param.5) | copy-start | bytes 1572868
  43.2 0.7 copy-start.3
  44.7 1.0 copy-start.1
  44.8 1.1 %copy-start.2 = (f32[1,1,256,512]{3,2,1,0:T(8,128)S(1)}, f32[1,1,256,512]{3,2,1,0:T(8,128)}, u32[]{:S(2)}) copy-start(f32[1,1,256,512]{3,2,1,0:T(8,128)} %param.7) | copy-start | bytes 1572868
  48.0 11.4 %collective-permute-start = (f32[256,512]{1,0:T(8,128)S(1)}, f32[256,512]{1,0:T(8,128)S(1)}, u32[]{:S(2)}, u32[]{:S(2)}) collective-permute-start(f32[256,512]{1,0:T(8,128)S(1)} %slice.25), channel_id=1, source_target_pairs={{0,1},{1,2},{2,3},{3,4},{4,5},{5,6},{6,7},{7,8},{8,9},{9,10},{10,1... | collective-permute-start | bytes 1572872 | tf_op jit(solution)/shard_map/ppermute | solution.py:12
  59.4 11.0 %collective-permute-start.1 = (f32[256,512]{1,0:T(8,128)S(1)}, f32[256,512]{1,0:T(8,128)S(1)}, u32[]{:S(2)}, u32[]{:S(2)}) collective-permute-start(f32[256,512]{1,0:T(8,128)S(1)} %slice_add_fusion), channel_id=1, source_target_pairs={{0,16},{1,17},{2,18},{3,19},{4,20},{5,21},{6,22},{7,23},{8,24},{9,... | collective-permute-start | bytes 1572872 | tf_op jit(solution)/shard_map/ppermute | solution.py:18
  72.0 11.1 %collective-permute-start.2 = (f32[256,512]{0,1:T(8,128)S(1)}, f32[256,512]{0,1:T(8,128)S(1)}, u32[]{:S(2)}, u32[]{:S(2)}) collective-permute-start(f32[256,512]{0,1:T(8,128)S(1)} %convolution_bitcast_fusion.1), channel_id=1, source_target_pairs={{16,0},{17,1},{18,2},{19,3},{20,4},{21,5},{22,6},{23,7},{24,8},{25... | collective-permute-start | bytes 1572872 | tf_op jit(solution)/shard_map/ppermute | solution.py:18
  83.1 13.2 %collective-permute-start.3 = (f32[256,512]{0,1:T(8,128)S(1)}, f32[256,512]{0,1:T(8,128)S(1)}, u32[]{:S(2)}, u32[]{:S(2)}) collective-permute-start(f32[256,512]{0,1:T(8,128)S(1)} %collective-permute-done.2), channel_id=1, source_target_pairs={{0,15},{1,0},{2,1},{3,2},{4,3},{5,4},{6,5},{7,6},{8,7},{9,8},{10,9... | collective-permute-start | bytes 1572872 | tf_op jit(solution)/shard_map/ppermute | solution.py:12
where the time goes:
time: 98.8 us; the launch traced here: 98.4 us
  blocking collectives  42 us (43%)
  waiting for transfers between devices  33.7 us (34%)
  starting transfers between devices  12 us (12%)
  matrix products  6.29 us (6%)
  local copies, waits for them, and re-layouts  3.03 us (3%)
  other arithmetic  1.25 us (1%)
    psum x1, blocking collectives, per_device(): norm_total = lax.psum(partial_value, ('level', 'sub'))  42 us
    ppermute x2, waiting for transfers between devices, passed_along(): return lax.ppermute(value, axis, pairs)  17.1 us
    ppermute x2, waiting for transfers between devices, shifted(): return lax.ppermute(block, axis, route)  16.5 us
    ppermute x2, starting transfers between devices, passed_along(): return lax.ppermute(value, axis, pairs)  6.51 us
    ppermute x2, starting transfers between devices, shifted(): return lax.ppermute(block, axis, route)  5.5 us
    dot_general x3, matrix products, apply_plain(): jnp.dot(matrix, values, precision=FULL_PRECISION, preferred_element_type=...  3.05 us
    dot_general x4, matrix products, apply_turned(): lax.dot_general(matrix, values, (((0,), (0,)), ((), ())), precision=FULL_...  2.35 us
  transfers between devices with their start and end apart: 4, of which 4 were waited for; matrix products, arithmetic and copies ran while one was open for 1% of the time, Pallas kernels for 0%

commit v1 on v0

--- a/solution.py
+++ b/solution.py
@@ -49,7 +49,7 @@
     next_rows = ordered[sn_width:]
     given_rhs = right_side[0, 0]
     partial_value = jnp.sum(given_rhs * given_rhs, axis=0)
-    norm_total = lax.psum(partial_value, ("level", "sub"))
+    norm_total = lax.psum(lax.psum(partial_value, "sub"), "level")
     col_scale = jnp.sqrt(norm_total / (levels * lax.axis_size("sub") * sn_width) + 1e-06)
     given_rhs = given_rhs / col_scale
     arrived = jnp.zeros_like(given_rhs)

time: 98.8 us -> 89.8 us (0.909)
  starting transfers between devices: 12 us -> 5.48 us
  blocking collectives: 42 us -> 39.8 us
    ppermute x2, starting transfers between devices: 6.51 us -> 0.72 us  [passed_along(): return lax.ppermute(value, axis, pairs)]
    psum x1 -> x2, blocking collectives: 42 us -> 39.8 us  [per_device(): norm_total = lax.psum(lax.psum(partial_value, 'sub'), 'level')]
where the time goes in v1:
time: 89.8 us; the launch traced here: 89.6 us
  blocking collectives  39.8 us (44%)
  waiting for transfers between devices  33.5 us (37%)
  matrix products  6.29 us (7%)
  starting transfers between devices  5.48 us (6%)
  local copies, waits for them, and re-layouts  3.03 us (3%)
  other arithmetic  1.25 us (1%)
    psum x2, blocking collectives, per_device(): norm_total = lax.psum(lax.psum(partial_value, 'sub'), 'level')  39.8 us
    ppermute x2, waiting for transfers between devices, passed_along(): return lax.ppermute(value, axis, pairs)  17.1 us
    ppermute x2, waiting for transfers between devices, shifted(): return lax.ppermute(block, axis, route)  16.4 us
    ppermute x2, starting transfers between devices, shifted(): return lax.ppermute(block, axis, route)  4.76 us
    dot_general x3, matrix products, apply_plain(): jnp.dot(matrix, values, precision=FULL_PRECISION, preferred_element_type=...  3.05 us
    dot_general x4, matrix products, apply_turned(): lax.dot_general(matrix, values, (((0,), (0,)), ((), ())), precision=FULL_...  2.36 us
  transfers between devices with their start and end apart: 4, of which 4 were waited for; matrix products, arithmetic and copies ran while one was open for 1% of the time, Pallas kernels for 0%

profile of v1, /device:TPU:0, one launch (start us, length us, event | category | flops | bytes accessed | tf_op | source)
XLA Modules:
  0.0 89.6 jit_solution(18203281529605066248)
XLA Ops:
  0.0 1.2 %fusion.5 = f32[512]{0:T(512)S(1)} fusion(f32[1,1,256,512]{3,2,1,0:T(8,128)} %param.7), kind=kLoop, calls=%fused_computation.12 | loop fusion | flops 261632 | bytes 526336 | tf_op jit(solution)/shard_map/reduce_sum | solution.py:51
  1.2 34.9 %psum.14 = f32[512]{0:T(512)S(1)} all-reduce(f32[512]{0:T(512)S(1)} %fusion.5), channel_id=1, replica_groups=mesh['level'=2,'sub'=16] {'sub'}, use_global_device_ids=true, to_apply=%region_1.0 | all-reduce | flops 512 | bytes 4096 | tf_op jit(solution)/shard_map/psum | solution.py:52
  36.1 4.9 %psum.15 = f32[512]{0:T(512)S(1)} all-reduce(f32[512]{0:T(512)S(1)} %psum.14), channel_id=1, replica_groups=mesh['level'=2,'sub'=16] {'level'}, use_global_device_ids=true, to_apply=%region_2.0 | all-reduce | flops 512 | bytes 4096 | tf_op jit(solution)/shard_map/psum | solution.py:52
  41.0 0.6 copy-done.3
  41.7 0.9 fusion.8
  42.6 0.1 copy.8
  42.7 0.8 copy-done.1
  43.5 0.2 copy-done.2
  43.7 1.0 %fusion.3 = f32[512,256]{1,0:T(8,128)S(1)} fusion(f32[1,1,256,512]{3,2,1,0:T(8,128)S(1)} %copy-done.2, f32[1,1,256,256]{3,2,1,0:T(8,128)S(1)} %copy-done.1, f32[512]{0:T(512)S(1)} %add_sqrt_fusion), kind=kOutput, calls=%fused_computation.8 | convolution fusion | flops 402784256 | bytes 1312768 | tf_op jit(solution)/shard_map/dot_general | solution.py:22
  44.7 1.0 %fusion.21 = f32[512,512]{1,0:T(8,128)S(1)} fusion(f32[512,256]{1,0:T(8,128)S(1)} %bitcast.49, f32[512,256]{1,0:T(8,128)S(1)} %fusion.3), kind=kOutput, calls=%fused_computation.28 | convolution fusion | flops 805306368 | bytes 2097152 | tf_op jit(solution)/shard_map/dot_general | solution.py:22
  45.8 11.3 %collective-permute-done = f32[256,512]{1,0:T(8,128)S(1)} collective-permute-done((f32[256,512]{1,0:T(8,128)S(1)}, f32[256,512]{1,0:T(8,128)S(1)}, u32[]{:S(2)}, u32[]{:S(2)}) %collective-permute-start) | collective-permute-done | bytes 524320 | tf_op jit(solution)/shard_map/ppermute | solution.py:12
  57.2 3.5 %collective-permute-start.1 = (f32[256,512]{1,0:T(8,128)S(1)}, f32[256,512]{1,0:T(8,128)S(1)}, u32[]{:S(2)}, u32[]{:S(2)}) collective-permute-start(f32[256,512]{1,0:T(8,128)S(1)} %slice_add_fusion), channel_id=1, source_target_pairs={{0,16},{1,17},{2,18},{3,19},{4,20},{5,21},{6,22},{7,23},{8,24},{9,... | collective-permute-start | bytes 1572872 | tf_op jit(solution)/shard_map/ppermute | solution.py:18
  60.7 6.6 %collective-permute-done.1 = f32[256,512]{1,0:T(8,128)S(1)} collective-permute-done((f32[256,512]{1,0:T(8,128)S(1)}, f32[256,512]{1,0:T(8,128)S(1)}, u32[]{:S(2)}, u32[]{:S(2)}) %collective-permute-start.1) | collective-permute-done | bytes 524320 | tf_op jit(solution)/shard_map/ppermute | solution.py:18
  67.3 1.0 %convolution_select_fusion = f32[512,256]{1,0:T(8,128)S(1)} fusion(f32[256,512]{1,0:T(8,128)S(1)} %collective-permute-done.1, f32[1,1,256,512]{3,2,1,0:T(8,128)S(1)} %copy-done.2, f32[512,256]{1,0:T(8,128)S(1)} %fusion.3, f32[1,1,256,256]{3,2,1,0:T(8,128)S(1)} %copy-done.1, f32[512]{0:T(512)S(1)} %add_sqrt_fusion, pred[]{:T(512)S(6)} %eq.23, pred[]{:T(512)S(6)} %eq.24), kind=kOutput, calls=%fused_computation.4 | convolution fusion | flops 403177472 | bytes 2361346 | tf_op jit(solution)/shard_map/dot_general | solution.py:22
  68.4 0.6 convolution_bitcast_fusion.1
  68.9 1.3 %collective-permute-start.2 = (f32[256,512]{0,1:T(8,128)S(1)}, f32[256,512]{0,1:T(8,128)S(1)}, u32[]{:S(2)}, u32[]{:S(2)}) collective-permute-start(f32[256,512]{0,1:T(8,128)S(1)} %convolution_bitcast_fusion.1), channel_id=1, source_target_pairs={{16,0},{17,1},{18,2},{19,3},{20,4},{21,5},{22,6},{23,7},{24,8},{25... | collective-permute-start | bytes 1572872 | tf_op jit(solution)/shard_map/ppermute | solution.py:18
  70.2 9.8 %collective-permute-done.2 = f32[256,512]{0,1:T(8,128)S(1)} collective-permute-done((f32[256,512]{0,1:T(8,128)S(1)}, f32[256,512]{0,1:T(8,128)S(1)}, u32[]{:S(2)}, u32[]{:S(2)}) %collective-permute-start.2) | collective-permute-done | bytes 524320 | tf_op jit(solution)/shard_map/ppermute | solution.py:18
  80.0 0.7 collective-permute-start.3
  80.7 0.2 fusion.20
  80.9 0.6 fusion.22
  81.5 5.8 %collective-permute-done.3 = f32[256,512]{0,1:T(8,128)S(1)} collective-permute-done((f32[256,512]{0,1:T(8,128)S(1)}, f32[256,512]{0,1:T(8,128)S(1)}, u32[]{:S(2)}, u32[]{:S(2)}) %collective-permute-start.3) | collective-permute-done | bytes 524320 | tf_op jit(solution)/shard_map/ppermute | solution.py:12
  87.4 0.6 fusion.2
  88.0 0.6 fusion.1
  88.6 1.0 %copy.11 = f32[1,1,256,512]{3,2,1,0:T(8,128)} copy(f32[1,1,256,512]{2,3,1,0:T(8,128)S(1)} %fusion.1) | data formatting | bytes 1048576 | tf_op jit(solution)/shard_map/broadcast_in_dim | solution.py:77
  (11 shorter events, 0.2 us)
Async XLA Ops:
  0.0 41.0 %copy-start = (f32[1,1,4,128,256]{4,3,2,1,0:T(8,128)S(1)}, f32[1,1,4,128,256]{4,3,2,1,0:T(8,128)}, u32[]{:S(2)}) copy-start(f32[1,1,4,128,256]{4,3,2,1,0:T(8,128)} %param.5) | copy-start | bytes 1572868
  41.0 0.7 copy-start.3
  42.5 1.0 %copy-start.1 = (f32[1,1,256,256]{3,2,1,0:T(8,128)S(1)}, f32[1,1,256,256]{3,2,1,0:T(8,128)}, u32[]{:S(2)}) copy-start(f32[1,1,256,256]{3,2,1,0:T(8,128)} %param.4) | copy-start | bytes 786436
  42.6 1.1 %copy-start.2 = (f32[1,1,256,512]{3,2,1,0:T(8,128)S(1)}, f32[1,1,256,512]{3,2,1,0:T(8,128)}, u32[]{:S(2)}) copy-start(f32[1,1,256,512]{3,2,1,0:T(8,128)} %param.7) | copy-start | bytes 1572868
  45.8 11.4 %collective-permute-start = (f32[256,512]{1,0:T(8,128)S(1)}, f32[256,512]{1,0:T(8,128)S(1)}, u32[]{:S(2)}, u32[]{:S(2)}) collective-permute-start(f32[256,512]{1,0:T(8,128)S(1)} %slice.25), channel_id=1, source_target_pairs={{0,1},{1,2},{2,3},{3,4},{4,5},{5,6},{6,7},{7,8},{8,9},{9,10},{10,1... | collective-permute-start | bytes 1572872 | tf_op jit(solution)/shard_map/ppermute | solution.py:12
  57.2 10.1 %collective-permute-start.1 = (f32[256,512]{1,0:T(8,128)S(1)}, f32[256,512]{1,0:T(8,128)S(1)}, u32[]{:S(2)}, u32[]{:S(2)}) collective-permute-start(f32[256,512]{1,0:T(8,128)S(1)} %slice_add_fusion), channel_id=1, source_target_pairs={{0,16},{1,17},{2,18},{3,19},{4,20},{5,21},{6,22},{7,23},{8,24},{9,... | collective-permute-start | bytes 1572872 | tf_op jit(solution)/shard_map/ppermute | solution.py:18
  68.9 11.1 %collective-permute-start.2 = (f32[256,512]{0,1:T(8,128)S(1)}, f32[256,512]{0,1:T(8,128)S(1)}, u32[]{:S(2)}, u32[]{:S(2)}) collective-permute-start(f32[256,512]{0,1:T(8,128)S(1)} %convolution_bitcast_fusion.1), channel_id=1, source_target_pairs={{16,0},{17,1},{18,2},{19,3},{20,4},{21,5},{22,6},{23,7},{24,8},{25... | collective-permute-start | bytes 1572872 | tf_op jit(solution)/shard_map/ppermute | solution.py:18
  80.0 7.4 %collective-permute-start.3 = (f32[256,512]{0,1:T(8,128)S(1)}, f32[256,512]{0,1:T(8,128)S(1)}, u32[]{:S(2)}, u32[]{:S(2)}) collective-permute-start(f32[256,512]{0,1:T(8,128)S(1)} %collective-permute-done.2), channel_id=1, source_target_pairs={{0,15},{1,0},{2,1},{3,2},{4,3},{5,4},{6,5},{7,6},{8,7},{9,8},{10,9... | collective-permute-start | bytes 1572872 | tf_op jit(solution)/shard_map/ppermute | solution.py:12
